TPU v7x, 256 devices: a whole 4x4x8 slice. The times are simulated.
256 devices in a mesh: row: 8 (over x_hi, y), col: 16 (over x_lo, z), depth: 2 (over core).
Axes of the slice: x: 4 (x_hi: 2, x_lo: 2; x = x_hi * 2 + x_lo), y: 4, z: 8, core: 2. Of those that a mesh axis runs over, the one named last changes fastest.
Arguments:
- snapshots: bfloat16 [8192, 6144], P('col', ('row', 'depth')), may hold values from -6 to 6
- cell_weight: float32 [6144], P(('row', 'depth')), may hold values from 0.25 to 4
Outputs:
- gram: float32 [8192, 8192], P('row', ('col', 'depth'))
All inputs are finite; a program needn't handle non-finite values.
Results may differ from a plain program's by a relative error of at most 0.0034.
Values may be sent and summed in bfloat16 or wider, within the bound.
A program may use at most 64 MiB of HBM per device.

v0:
```python
import jax
import jax.numpy as jnp
from jax import lax
from jax.sharding import PartitionSpec as P

CELLS = 6144


def spread(value, axis, root):
    mine = lax.axis_index(axis) == root
    return lax.psum(jnp.where(mine, value, jnp.zeros_like(value)), axis)


def block_product(left_rows, right_rows):
    return lax.dot_general(
        left_rows, right_rows, (((1,), (1,)), ((), ())), preferred_element_type=jnp.float32
    )


def on_device(snapshots, cell_weight):
    root_weight = jnp.sqrt(cell_weight)
    scaled = (snapshots.astype(jnp.float32) * root_weight[None, :]).astype(jnp.bfloat16)
    ratio = lax.axis_size("col") // lax.axis_size("row")
    row_index = lax.axis_index("row")
    own_half = lax.all_to_all(scaled, "depth", split_axis=0, concat_axis=1, tiled=True)
    column_rows = lax.all_gather(own_half, "row", axis=1, tiled=True)
    blocks = []
    for offset in range(ratio):
        received = spread(column_rows, "col", row_index * ratio + offset)
        panel = lax.all_gather(received, "depth", axis=0, tiled=True)
        blocks.append(block_product(panel, column_rows))
    summed = jnp.concatenate(blocks, axis=0)
    return summed / jnp.float32(CELLS)


def solution(mesh):
    return jax.shard_map(
        on_device,
        mesh=mesh,
        in_specs=(P("col", ("row", "depth")), P(("row", "depth"))),
        out_specs=P("row", ("col", "depth")),
        check_vma=False,
    )
```

profile of v0, /device:TPU:1, one launch (start us, length us, event | category | flops | bytes accessed | tf_op | source)
XLA Modules:
  0.0 312.5 jit_solution(17423698580459638901)
XLA Ops:
  6.5 0.0 all-gather.4.cloned.1.call-start
  6.5 0.7 sqrt.3
  7.2 1.1 multiply_convert_fusion
  8.3 6.9 %all_to_all.19 = bf16[2,256,384]{2,1,0:T(8,128)(2,1)S(1)} all-to-all(bf16[2,256,384]{2,1,0:T(8,128)(2,1)S(1)} %bitcast.8), channel_id=1, replica_groups=mesh['row'=8,'col'=16,'depth'=2] {'depth'}, dimensions={0} | all-to-all | bytes 786432 | tf_op jit(solution)/shard_map/all_to_all | solution.py:25
  15.2 0.9 copy.3
  16.1 0.0 all-gather.4.cloned.1.call-update
  16.2 0.0 all-reduce.3.cloned.1.call-start
  16.2 68.3 %all-gather.4.cloned.1.call-done = bf16[256,6144]{0,1:T(8,128)(2,1)} async-done(((bf16[256,768]{0,1:T(8,128)(2,1)}), bf16[256,6144]{0,1:T(8,128)(2,1)}) %all-gather.4.cloned.1.call-update) | async-done | bytes 3145744 | tf_op jit(solution)/shard_map/all_gather | solution.py:26
  84.6 4.9 %broadcast_select_fusion.1 = (bf16[256,6144]{0,1:T(8,128)(2,1)}, bf16[256,6144]{0,1:T(8,128)(2,1)}) fusion(bf16[256,6144]{0,1:T(8,128)(2,1)} %all-gather.4.cloned.1.call-done, pred[]{:T(512)S(6)} %eq.6, pred[]{:T(512)S(6)} %eq.7), kind=kLoop, calls=%fused_computation.1 | loop fusion | flops 3145728 | bytes 9437186 | tf_op jit(solution)/shard_map/jit(_where)/select_n | solution.py:11
  89.5 0.0 all-reduce.3.cloned.1.call-update
  89.5 0.0 all-gather.8.cloned.1.call-start
  89.6 162.2 %all-reduce.3.cloned.1.call-done = (bf16[256,6144]{0,1:T(8,128)(2,1)}, bf16[256,6144]{0,1:T(8,128)(2,1)}) async-done(((bf16[256,6144]{0,1:T(8,128)(2,1)}, bf16[256,6144]{0,1:T(8,128)(2,1)}), (bf16[256,6144]{0,1:T(8,128)(2,1)}, bf16[256,6144]{0,1:T(8,128)(2,1)})) %all-reduce.3.cloned.1.call-update) | async-done | bytes 6291472 | tf_op jit(solution)/shard_map/psum | solution.py:11
  251.7 0.0 copy-start
  251.7 0.0 all-gather.8.cloned.1.call-update
  251.8 0.0 all-gather.6.cloned.1.call-start
  251.8 0.5 all-gather.6.cloned.1.call-update
  252.3 23.9 %all-gather.8.cloned.1.call-done = bf16[512,6144]{0,1:T(8,128)(2,1)} async-done(((bf16[256,6144]{0,1:T(8,128)(2,1)}), bf16[512,6144]{0,1:T(8,128)(2,1)}) %all-gather.8.cloned.1.call-update) | async-done | bytes 6291472 | tf_op jit(solution)/shard_map/all_gather | solution.py:30
  276.3 0.0 copy-done
  276.3 5.4 %fusion.1 = f32[512,256]{1,0:T(8,128)} fusion(bf16[512,6144]{0,1:T(8,128)(2,1)} %all-gather.8.cloned.1.call-done, bf16[256,6144]{0,1:T(8,128)(2,1)S(1)} %copy-done), kind=kOutput, calls=%fused_computation.5 | convolution fusion | flops 1610612736 | bytes 9961472 | tf_op jit(solution)/shard_map/dot_general | solution.py:15
  281.7 18.6 %all-gather.6.cloned.1.call-done = bf16[512,6144]{0,1:T(8,128)(2,1)} async-done(((bf16[256,6144]{0,1:T(8,128)(2,1)}), bf16[512,6144]{0,1:T(8,128)(2,1)}) %all-gather.6.cloned.1.call-update) | async-done | bytes 6291472 | tf_op jit(solution)/shard_map/all_gather | solution.py:30
  300.2 0.0 copy-start.1
  300.2 4.7 %fusion = f32[512,256]{1,0:T(8,128)S(1)} fusion(bf16[512,6144]{0,1:T(8,128)(2,1)} %all-gather.6.cloned.1.call-done, bf16[256,6144]{0,1:T(8,128)(2,1)S(1)} %copy-done), kind=kOutput, calls=%fused_computation.4 | convolution fusion | flops 1610612736 | bytes 9961472 | tf_op jit(solution)/shard_map/dot_general | solution.py:15
  304.9 0.0 copy-done.1
  304.9 1.1 maximum_multiply_fusion
Async XLA Ops:
  6.5 78.0 %all-gather.4.cloned.1.call-start = ((), (), s32[]{:S(2)}) async-start(), calls=%async_computation.1 | async-start | bytes 3538944 | tf_op jit(solution)/shard_map/all_gather | solution.py:26
  16.2 235.6 %all-reduce.3.cloned.1.call-start = ((), (), s32[]{:S(2)}) async-start(), calls=%async_computation.4 | async-start | bytes 12582912 | tf_op jit(solution)/shard_map/psum | solution.py:11
  89.5 186.7 %all-gather.8.cloned.1.call-start = ((), (), s32[]{:S(2)}) async-start(), calls=%async_computation.3 | async-start | bytes 9437184 | tf_op jit(solution)/shard_map/all_gather | solution.py:30
  251.7 24.5 %copy-start = (bf16[256,6144]{0,1:T(8,128)(2,1)S(1)}, bf16[256,6144]{0,1:T(8,128)(2,1)}, u32[]{:S(2)}) copy-start(bf16[256,6144]{0,1:T(8,128)(2,1)} %all-gather.4.cloned.1.call-done) | copy-start | bytes 9437188
  251.8 48.5 %all-gather.6.cloned.1.call-start = ((), (), s32[]{:S(2)}) async-start(), calls=%async_computation.2 | async-start | bytes 9437184 | tf_op jit(solution)/shard_map/all_gather | solution.py:30
  300.2 4.7 %copy-start.1 = (f32[512,256]{1,0:T(8,128)S(1)}, f32[512,256]{1,0:T(8,128)}, u32[]{:S(2)}) copy-start(f32[512,256]{1,0:T(8,128)} %fusion.1) | copy-start | bytes 1572868
Sparse Core Ops, SparseCore 0:
  16.3 68.2 all-gather.3
  89.6 162.0 all-reduce.2
  253.5 22.6 all-gather.7
  277.9 22.2 all-gather.5
where the time goes:
time: 313 us
  waiting for transfers between devices  274 us (88%)
  between operations  13.2 us (4%)
  matrix products  10.1 us (3%)
  other arithmetic  7.09 us (2%)
  blocking collectives  6.92 us (2%)
    psum x1, waiting for transfers between devices, spread(): return lax.psum(jnp.where(mine, value, jnp.zeros_like(value)), axis)  162 us
    all_gather x1, waiting for transfers between devices, on_device(): column_rows = lax.all_gather(own_half, 'row', axis=1, tiled=True)  68.3 us
    all_gather x2, waiting for transfers between devices, on_device(): panel = lax.all_gather(received, 'depth', axis=0, tiled=True)  42.5 us
    dot_general x2, matrix products, block_product(): lax.dot_general(left_rows, right_rows, (((1,), (1,)), ((), ())), preferre...  10.1 us
    all_to_all x1, blocking collectives, on_device(): lax.all_to_all(scaled, 'depth', split_axis=0, concat_axis=1, tiled=True)  6.92 us
  transfers between devices with their start and end apart: 4, of which 4 were waited for; matrix products, arithmetic and copies ran while one was open for 2% of the time, Pallas kernels for 0%

commit v1 on v0

--- a/solution.py
+++ b/solution.py
@@ -23,7 +23,9 @@
     ratio = lax.axis_size("col") // lax.axis_size("row")
     row_index = lax.axis_index("row")
     own_half = lax.all_to_all(scaled, "depth", split_axis=0, concat_axis=1, tiled=True)
-    column_rows = lax.all_gather(own_half, "row", axis=1, tiled=True)
+    column_rows = jnp.concatenate(
+        lax.all_to_all(jnp.stack([own_half] * lax.axis_size("row")), "row", 0, 0), axis=1
+    )
     blocks = []
     for offset in range(ratio):
         received = spread(column_rows, "col", row_index * ratio + offset)

time: 313 us -> 293 us (0.936)
  waiting for transfers between devices: 274 us -> 246 us
  starting transfers between devices: 0.12 us -> 5.03 us
  local copies, waits for them, and re-layouts: 1.62 us -> 6.08 us
    all_gather x1 -> x0, waiting for transfers between devices: 68.3 us -> none  [on_device(): column_rows = lax.all_gather(own_half, 'row', axis=1, tiled=True)]
    all_to_all x0 -> x1, waiting for transfers between devices: none -> 37.5 us  [on_device(): lax.all_to_all(jnp.stack([own_half] * lax.axis_size('row')), 'row', 0, 0)]
    all_to_all x0 -> x1, starting transfers between devices: none -> 4.91 us  [on_device(): lax.all_to_all(jnp.stack([own_half] * lax.axis_size('row')), 'row', 0, 0)]
    all_to_all x0 -> x1, local copies, waits for them, and re-layouts: none -> 3.17 us  [on_device(): lax.all_to_all(jnp.stack([own_half] * lax.axis_size('row')), 'row', 0, 0)]
where the time goes in v1:
time: 293 us; the launch traced here: 292 us
  waiting for transfers between devices  246 us (84%)
  between operations  13.2 us (5%)
  matrix products  10.1 us (3%)
  blocking collectives  6.92 us (2%)
  local copies, waits for them, and re-layouts  6.08 us (2%)
  other arithmetic  5.41 us (2%)
  starting transfers between devices  5.03 us (2%)
    psum x1, waiting for transfers between devices, spread(): return lax.psum(jnp.where(mine, value, jnp.zeros_like(value)), axis)  165 us
    all_gather x2, waiting for transfers between devices, on_device(): panel = lax.all_gather(received, 'depth', axis=0, tiled=True)  42.5 us
    all_to_all x1, waiting for transfers between devices, on_device(): lax.all_to_all(jnp.stack([own_half] * lax.axis_size('row')), 'row', 0, 0)  37.5 us
    dot_general x2, matrix products, block_product(): lax.dot_general(left_rows, right_rows, (((1,), (1,)), ((), ())), preferre...  10.1 us
    all_to_all x1, blocking collectives, on_device(): lax.all_to_all(scaled, 'depth', split_axis=0, concat_axis=1, tiled=True)  6.92 us
  transfers between devices with their start and end apart: 4, of which 4 were waited for; matrix products, arithmetic and copies ran while one was open for 2% of the time, Pallas kernels for 0%

profile of v1, /device:TPU:1, one launch (start us, length us, event | category | flops | bytes accessed | tf_op | source)
XLA Modules:
  0.0 292.4 jit_solution(4409419903419167150)
XLA Ops:
  6.5 0.7 sqrt.3
  7.2 1.1 multiply_convert_fusion
  8.3 6.9 %all_to_all.21 = bf16[2,256,384]{2,1,0:T(8,128)(2,1)S(1)} all-to-all(bf16[2,256,384]{2,1,0:T(8,128)(2,1)S(1)} %bitcast.14), channel_id=1, replica_groups=mesh['row'=8,'col'=16,'depth'=2] {'depth'}, dimensions={0} | all-to-all | bytes 786432 | tf_op jit(solution)/shard_map/all_to_all | solution.py:25
  15.2 0.2 copy.8
  15.4 0.2 copy.9
  15.6 1.9 stack.5
  17.5 4.9 %all-to-all-start.1 = ((bf16[8,256,768]{2,1,0:T(8,128)(2,1)}), bf16[8,256,768]{2,1,0:T(8,128)(2,1)}, u32[]{:S(2)}, u32[]{:S(2)}) async-start(bf16[8,256,768]{2,1,0:T(8,128)(2,1)} %stack.5), calls=%async_computation.1 | async-start | bytes 6291456 | tf_op jit(solution)/shard_map/all_to_all | solution.py:27
  22.4 0.0 all-reduce.3.cloned.1.call-start
  22.4 37.5 %all-to-all-done.1 = bf16[8,256,768]{2,1,0:T(8,128)(2,1)} async-done(((bf16[8,256,768]{2,1,0:T(8,128)(2,1)}), bf16[8,256,768]{2,1,0:T(8,128)(2,1)}, u32[]{:S(2)}, u32[]{:S(2)}) %all-to-all-start.1) | async-done | bytes 3145760 | tf_op jit(solution)/shard_map/all_to_all | solution.py:27
  59.9 3.2 %copy.10 = bf16[8,256,768]{1,2,0:T(8,128)(2,1)S(1)} copy(bf16[8,256,768]{2,1,0:T(8,128)(2,1)} %all-to-all-done.1) | data formatting | bytes 6291456 | tf_op jit(solution)/shard_map/all_to_all | solution.py:27
  63.1 3.3 %broadcast_select_fusion.1 = (bf16[256,6144]{0,1:T(8,128)(2,1)}, bf16[256,6144]{0,1:T(8,128)(2,1)}) fusion(pred[]{:T(512)S(6)} %eq.6, bf16[8,256,768]{1,2,0:T(8,128)(2,1)S(1)} %copy.10, pred[]{:T(512)S(6)} %eq.7), kind=kLoop, calls=%fused_computation.1 | loop fusion | flops 3145728 | bytes 9437186 | tf_op jit(solution)/shard_map/jit(_where)/select_n | solution.py:11
  66.3 0.0 all-reduce.3.cloned.1.call-update
  66.4 0.0 all-gather.5.cloned.1.call-start
  66.4 165.1 %all-reduce.3.cloned.1.call-done = (bf16[256,6144]{0,1:T(8,128)(2,1)}, bf16[256,6144]{0,1:T(8,128)(2,1)}) async-done(((bf16[256,6144]{0,1:T(8,128)(2,1)}, bf16[256,6144]{0,1:T(8,128)(2,1)}), (bf16[256,6144]{0,1:T(8,128)(2,1)}, bf16[256,6144]{0,1:T(8,128)(2,1)})) %all-reduce.3.cloned.1.call-update) | async-done | bytes 6291472 | tf_op jit(solution)/shard_map/psum | solution.py:11
  231.5 0.0 all-gather.5.cloned.1.call-update
  231.5 0.0 all-gather.3.cloned.1.call-start
  231.5 0.7 all-gather.3.cloned.1.call-update
  232.2 23.8 %all-gather.5.cloned.1.call-done = bf16[512,6144]{0,1:T(8,128)(2,1)} async-done(((bf16[256,6144]{0,1:T(8,128)(2,1)}), bf16[512,6144]{0,1:T(8,128)(2,1)}) %all-gather.5.cloned.1.call-update) | async-done | bytes 6291472 | tf_op jit(solution)/shard_map/all_gather | solution.py:32
  256.0 5.4 %fusion.1 = f32[512,256]{1,0:T(8,128)} fusion(bf16[512,6144]{0,1:T(8,128)(2,1)} %all-gather.5.cloned.1.call-done, bf16[256,6144]{0,1:T(8,128)(2,1)S(1)} %bitcast.12), kind=kOutput, calls=%fused_computation.5 | convolution fusion | flops 1610612736 | bytes 9961472 | tf_op jit(solution)/shard_map/dot_general | solution.py:15
  261.4 18.7 %all-gather.3.cloned.1.call-done = bf16[512,6144]{0,1:T(8,128)(2,1)} async-done(((bf16[256,6144]{0,1:T(8,128)(2,1)}), bf16[512,6144]{0,1:T(8,128)(2,1)}) %all-gather.3.cloned.1.call-update) | async-done | bytes 6291472 | tf_op jit(solution)/shard_map/all_gather | solution.py:32
  280.1 0.0 copy-start
  280.1 4.7 %fusion = f32[512,256]{1,0:T(8,128)S(1)} fusion(bf16[512,6144]{0,1:T(8,128)(2,1)} %all-gather.3.cloned.1.call-done, bf16[256,6144]{0,1:T(8,128)(2,1)S(1)} %bitcast.13), kind=kOutput, calls=%fused_computation.4 | convolution fusion | flops 1610612736 | bytes 9961472 | tf_op jit(solution)/shard_map/dot_general | solution.py:15
  284.8 0.0 copy-done
  284.8 1.1 maximum_multiply_fusion
Async XLA Ops:
  17.5 42.4 %all-to-all-start.1 = ((bf16[8,256,768]{2,1,0:T(8,128)(2,1)}), bf16[8,256,768]{2,1,0:T(8,128)(2,1)}, u32[]{:S(2)}, u32[]{:S(2)}) async-start(bf16[8,256,768]{2,1,0:T(8,128)(2,1)} %stack.5), calls=%async_computation.1 | async-start | bytes 6291456 | tf_op jit(solution)/shard_map/all_to_all | solution.py:27
  22.4 209.1 %all-reduce.3.cloned.1.call-start = ((), (), s32[]{:S(2)}) async-start(), calls=%async_computation.4 | async-start | bytes 12582912 | tf_op jit(solution)/shard_map/psum | solution.py:11
  66.4 189.6 %all-gather.5.cloned.1.call-start = ((), (), s32[]{:S(2)}) async-start(), calls=%async_computation.3 | async-start | bytes 9437184 | tf_op jit(solution)/shard_map/all_gather | solution.py:32
  231.5 48.6 %all-gather.3.cloned.1.call-start = ((), (), s32[]{:S(2)}) async-start(), calls=%async_computation.2 | async-start | bytes 9437184 | tf_op jit(solution)/shard_map/all_gather | solution.py:32
  280.1 4.7 %copy-start = (f32[512,256]{1,0:T(8,128)S(1)}, f32[512,256]{1,0:T(8,128)}, u32[]{:S(2)}) copy-start(f32[512,256]{1,0:T(8,128)} %fusion.1) | copy-start | bytes 1572868
Sparse Core Ops, SparseCore 0:
  66.5 164.9 all-reduce.2
  233.3 22.6 all-gather.4
  257.8 22.2 all-gather.2
